TPU v7x, 32 devices: a whole 2x2x4 slice. The times are simulated.
32 devices in a mesh: groups: 2 (over y), ctx: 4 (over z), head: 2 (over x), dp: 2 (over core).
Axes of the slice: x: 2, y: 2, z: 4, core: 2. Of those that a mesh axis runs over, the one named last changes fastest.
Arguments:
- queries: bfloat16 [4, 4, 512, 16, 128], P(('groups', 'dp'), 'ctx', None, 'head'), parts along dimension 0, may hold values from -6 to 6
- key_vecs: bfloat16 [4, 4, 512, 16, 128], P(('groups', 'dp'), 'ctx', None, 'head'), parts along dimension 0, may hold values from -6 to 6
- value_vecs: bfloat16 [4, 4, 512, 16, 128], P(('groups', 'dp'), 'ctx', None, 'head'), parts along dimension 0, may hold values from -6 to 6
- grad_out: bfloat16 [4, 4, 512, 16, 128], P(('groups', 'dp'), 'ctx', None, 'head'), parts along dimension 0, may hold values from -6 to 6
Outputs:
- attended: bfloat16 [4, 4, 512, 16, 128], P(('groups', 'dp'), 'ctx', None, 'head'), parts along dimension 0
- grad_queries: bfloat16 [4, 4, 512, 16, 128], P(('groups', 'dp'), 'ctx', None, 'head'), parts along dimension 0
- grad_keys: bfloat16 [4, 4, 512, 16, 128], P(('groups', 'dp'), 'ctx', None, 'head'), parts along dimension 0
- grad_values: bfloat16 [4, 4, 512, 16, 128], P(('groups', 'dp'), 'ctx', None, 'head'), parts along dimension 0
There are 2 independent parts, one for each index of `groups`. A program takes and returns all parts, laid end to end along the dimension named above; each array names one. Nothing has to cross between parts.
All inputs are finite; a program needn't handle non-finite values.
Results may differ from a plain program's by a relative error of at most 0.013.
Values may be sent and summed in bfloat16 or wider, within the bound.
A program may use at most 128 MiB of HBM per device.

v0:
```python
import math

import jax
import jax.numpy as jnp
from jax import lax
from jax.sharding import PartitionSpec as P


def causal(length):
    positions = jnp.arange(length)
    return positions[None, :] <= positions[:, None]


def attend(query_in, key_in, value_in, grad_in, layout, allowed):
    scaling = 1.0 / math.sqrt(query_in.shape[-1])
    key_form = layout.replace("q", "k")
    scores = (
        jnp.einsum(
            layout + "," + key_form + "->bxhqk",
            query_in,
            key_in,
            preferred_element_type=jnp.float32,
        )
        * scaling
    )
    scores = jnp.where(allowed, scores, -1e30)
    highest = jnp.max(scores, axis=-1, keepdims=True)
    weight_sum = jnp.sum(jnp.exp(scores - highest), axis=-1, keepdims=True)
    log_total = highest + jnp.log(weight_sum)
    weights = jnp.where(allowed, jnp.exp(scores - log_total), 0.0)
    rounded = weights.astype(jnp.bfloat16)
    output = jnp.einsum(
        "bxhqk," + key_form + "->" + layout, rounded, value_in, preferred_element_type=jnp.float32
    ).astype(jnp.bfloat16)
    row_dots = jnp.einsum(
        layout + "," + layout + "->bxhq", grad_in, output, preferred_element_type=jnp.float32
    )
    dprobs = jnp.einsum(
        layout + "," + key_form + "->bxhqk", grad_in, value_in, preferred_element_type=jnp.float32
    )
    dscores = (weights * (dprobs - row_dots[..., None]) * scaling).astype(jnp.bfloat16)
    grad_query = jnp.einsum(
        "bxhqk," + key_form + "->" + layout, dscores, key_in, preferred_element_type=jnp.float32
    ).astype(jnp.bfloat16)
    grad_key = jnp.einsum(
        "bxhqk," + layout + "->" + key_form, dscores, query_in, preferred_element_type=jnp.float32
    )
    grad_value = jnp.einsum(
        "bxhqk," + layout + "->" + key_form, rounded, grad_in, preferred_element_type=jnp.float32
    )
    return (output, grad_query, grad_key, grad_value)


def merge_heads(first_part, second_part):
    stacked = jnp.stack((first_part, second_part), axis=4)
    shape = first_part.shape
    return stacked.reshape(shape[:3] + (2 * shape[3], shape[4]))


def per_device(queries, key_vecs, value_vecs, grad_out):
    arrays = (queries, key_vecs, value_vecs, grad_out)
    row_parts = tuple((array[:, :, :, 0::2] for array in arrays))
    col_parts = tuple((array[:, :, :, 1::2] for array in arrays))
    row_local = attend(
        row_parts[0], row_parts[1], row_parts[2], row_parts[3], "bxqhd", causal(queries.shape[2])
    )
    row_results = (
        row_local[0],
        row_local[1],
        row_local[2].astype(jnp.bfloat16),
        row_local[3].astype(jnp.bfloat16),
    )
    local_rows = col_parts[0].shape[1]
    gathered = (
        lax.all_gather(col_parts[1], "ctx", axis=1, tiled=True),
        lax.all_gather(col_parts[2], "ctx", axis=1, tiled=True),
    )
    query_rows = lax.axis_index("ctx") * local_rows + jnp.arange(local_rows)
    key_rows = jnp.arange(gathered[0].shape[1])
    allowed = key_rows[None, :] <= query_rows[:, None]
    col_local = attend(col_parts[0], gathered[0], gathered[1], col_parts[3], "bqxhd", allowed)
    summed = (
        lax.psum_scatter(col_local[2], "ctx", scatter_dimension=1, tiled=True),
        lax.psum_scatter(col_local[3], "ctx", scatter_dimension=1, tiled=True),
    )
    col_results = (
        col_local[0],
        col_local[1],
        summed[0].astype(jnp.bfloat16),
        summed[1].astype(jnp.bfloat16),
    )
    return (
        merge_heads(row_results[0], col_results[0]),
        merge_heads(row_results[1], col_results[1]),
        merge_heads(row_results[2], col_results[2]),
        merge_heads(row_results[3], col_results[3]),
    )


def solution(mesh):
    placed = (
        P(("groups", "dp"), "ctx", None, "head", None),
        P(("groups", "dp"), "ctx", None, "head", None),
        P(("groups", "dp"), "ctx", None, "head", None),
        P(("groups", "dp"), "ctx", None, "head", None),
    )
    return jax.shard_map(
        per_device,
        mesh=mesh,
        in_specs=placed,
        out_specs=(
            P(("groups", "dp"), "ctx", None, "head", None),
            P(("groups", "dp"), "ctx", None, "head", None),
            P(("groups", "dp"), "ctx", None, "head", None),
            P(("groups", "dp"), "ctx", None, "head", None),
        ),
        check_vma=False,
    )
```

profile of v0, /device:TPU:0, one launch (start us, length us, event | category | flops | bytes accessed | tf_op | source)
XLA Modules:
  0.0 279.8 jit_solution(17186343731530669740)
XLA Ops:
  7.2 9.0 %slice.28 = bf16[1,1,512,4,128]{4,3,2,1,0:T(4,128)(2,1)S(1)} slice(bf16[1,1,512,8,128]{4,3,2,1,0:T(8,128)(2,1)} %param.5), slice={[0:1:1], [0:1:1], [0:512:1], [1:8:2], [0:128:1]} | slice | bytes 1048576 | tf_op jit(solution)/shard_map/slice | solution.py:63
  16.3 0.9 copy.80
  17.2 8.9 %slice.29 = bf16[1,1,512,4,128]{4,3,2,1,0:T(4,128)(2,1)S(1)} slice(bf16[1,1,512,8,128]{4,3,2,1,0:T(8,128)(2,1)} %param.6), slice={[0:1:1], [0:1:1], [0:512:1], [1:8:2], [0:128:1]} | slice | bytes 1048576 | tf_op jit(solution)/shard_map/slice | solution.py:63
  26.1 0.9 copy.81
  27.0 2.2 slice.31
  29.2 2.2 slice.27
  31.4 0.1 bitcast_convert_fusion.2
  31.6 34.3 %all-gather.3.cloned.1.call-done = bf16[1,4,512,4,128]{4,2,3,0,1:T(8,128)(2,1)} async-done(((bf16[1,1,512,4,128]{4,2,3,0,1:T(8,128)(2,1)}), bf16[1,4,512,4,128]{4,2,3,0,1:T(8,128)(2,1)}) %all-gather.3.cloned.1.call-update) | async-done | bytes 2097168 | tf_op jit(solution)/shard_map/all_gather | solution.py:75
  66.0 5.0 %fusion.8 = f32[512,4,1,4]{3,2,1,0:T(1,128)} fusion(bf16[4,512,4,128]{3,1,2,0:T(8,128)(2,1)} %bitcast.148, bf16[512,4,128,1]{2,1,0,3:T(4,128)(2,1)S(1)} %bitcast.143), kind=kOutput, calls=%fused_computation.14 | convolution fusion | flops 2097152 | bytes 2654208 | tf_op jit(solution)/shard_map/bqxhd,bkxhd->bxhqk/dot_general | solution.py:18
  70.9 2.2 copy.56
  73.2 0.1 fusion.29
  73.5 3.1 %multiply_bitcast_fusion = f32[1,4,512,4,128]{4,2,3,1,0:T(8,128)} fusion(f32[512,4,128]{2,0,1:T(8,128)S(1)} %copy.47, f32[512,4,4]{0,1,2:T(4,128)S(1)} %get-tuple-element.12), kind=kLoop, calls=%fused_computation | loop fusion | flops 1048576 | bytes 5275648 | tf_op jit(solution)/shard_map/bxhqk,bqxhd->bkxhd/transpose | solution.py:48
  76.7 0.1 bitcast_convert_fusion.3
  76.9 35.9 %all-gather.5.cloned.1.call-done = bf16[1,4,512,4,128]{4,2,3,0,1:T(8,128)(2,1)} async-done(((bf16[1,1,512,4,128]{4,2,3,0,1:T(8,128)(2,1)}), bf16[1,4,512,4,128]{4,2,3,0,1:T(8,128)(2,1)}) %all-gather.5.cloned.1.call-update) | async-done | bytes 2097168 | tf_op jit(solution)/shard_map/all_gather | solution.py:76
  112.8 5.0 %fusion.2 = f32[512,4,1,4]{3,2,1,0:T(1,128)} fusion(bf16[4,512,4,128]{3,1,2,0:T(8,128)(2,1)} %bitcast.150, bf16[512,4,128,1]{2,1,0,3:T(4,128)(2,1)S(1)} %bitcast.138), kind=kOutput, calls=%fused_computation.8 | convolution fusion | flops 2097152 | bytes 2654208 | tf_op jit(solution)/shard_map/bqxhd,bkxhd->bxhqk/dot_general | solution.py:38
  117.7 2.3 copy.69
  120.0 2.0 copy.57
  122.1 4.4 %fusion.4 = bf16[512,4,1,128]{3,2,1,0:T(2,128)(2,1)S(1)} fusion(bf16[512,4,4,1]{2,3,1,0:T(2,128)(2,1)} %copy.57, bf16[4,512,4,128]{3,1,2,0:T(8,128)(2,1)} %bitcast.151), kind=kOutput, calls=%fused_computation.10 | convolution fusion | flops 2097152 | bytes 2637824 | tf_op jit(solution)/shard_map/bxhqk,bkxhd->bqxhd/dot_general | solution.py:32
  126.5 0.1 fusion.22
  126.6 0.9 multiply_reduce_fusion
  127.5 0.1 copy.73
  127.6 0.1 fusion.34
  127.7 3.1 %multiply_bitcast_fusion.1 = f32[1,4,512,4,128]{4,2,3,1,0:T(8,128)} fusion(f32[512,4,128]{2,0,1:T(8,128)S(1)} %copy.45, f32[512,4,4]{0,1,2:T(4,128)S(1)} %get-tuple-element.14), kind=kLoop, calls=%fused_computation.1 | loop fusion | flops 1048576 | bytes 5275648 | tf_op jit(solution)/shard_map/bxhqk,bqxhd->bkxhd/transpose | solution.py:45
  130.9 2.2 slice.30
  133.1 6.7 %slice.24 = bf16[1,1,512,4,128]{4,3,2,1,0:T(4,128)(2,1)} slice(bf16[1,1,512,8,128]{4,3,2,1,0:T(8,128)(2,1)S(1)} %copy-done.2), slice={[0:1:1], [0:1:1], [0:512:1], [0:8:2], [0:128:1]} | slice | bytes 1048576 | tf_op jit(solution)/shard_map/slice | solution.py:62
  139.8 8.9 %slice.25 = bf16[1,1,512,4,128]{4,3,2,1,0:T(4,128)(2,1)S(1)} slice(bf16[1,1,512,8,128]{4,3,2,1,0:T(8,128)(2,1)} %param.5), slice={[0:1:1], [0:1:1], [0:512:1], [0:8:2], [0:128:1]} | slice | bytes 1048576 | tf_op jit(solution)/shard_map/slice | solution.py:62
  148.7 9.1 %slice.26 = bf16[1,1,512,4,128]{4,3,2,1,0:T(4,128)(2,1)S(1)} slice(bf16[1,1,512,8,128]{4,3,2,1,0:T(8,128)(2,1)} %param.6), slice={[0:1:1], [0:1:1], [0:512:1], [0:8:2], [0:128:1]} | slice | bytes 1048576 | tf_op jit(solution)/shard_map/slice | solution.py:62
  157.8 2.0 fusion.1
  159.8 0.9 exponential_reduce_fusion
  160.8 2.5 fusion.13
  163.2 1.7 multiply_convert_fusion
  165.0 0.9 fusion.10
  165.9 1.5 fusion.11
  167.4 1.3 fusion.12
  168.8 1.1 copy.74
  169.8 4.0 %fusion.6 = bf16[512,4,1,128]{3,2,1,0:T(2,128)(2,1)S(1)} fusion(bf16[512,4,4,1]{2,3,1,0:T(2,128)(2,1)S(1)} %copy.74, bf16[4,512,4,128]{3,1,2,0:T(8,128)(2,1)} %bitcast.149), kind=kOutput, calls=%fused_computation.12 | convolution fusion | flops 2097152 | bytes 2637824 | tf_op jit(solution)/shard_map/bxhqk,bkxhd->bqxhd/dot_general | solution.py:42
  174.0 0.1 pad_maximum_fusion.1
  174.2 1.6 copy.50
  175.8 0.1 pad_maximum_fusion
  176.0 1.6 copy.49
  177.7 12.9 %reduce-scatter.5.cloned.1.call-done = f32[1,1,512,4,128]{4,2,3,1,0:T(8,128)} async-done(((f32[1,4,512,4,128]{4,2,3,1,0:T(8,128)}), f32[1,1,512,4,128]{4,2,3,1,0:T(8,128)}) %reduce-scatter.5.cloned.1.call-update) | async-done | bytes 1048592 | tf_op jit(solution)/shard_map/reduce_scatter | solution.py:84
  190.6 1.3 convert_bitcast_fusion
  191.9 0.1 pad_maximum_fusion.3
  192.1 1.6 copy.52
  193.7 76.4 %reduce-scatter.3.cloned.1.call-done = f32[1,1,512,4,128]{4,2,3,1,0:T(8,128)} async-done(((f32[1,4,512,4,128]{4,2,3,1,0:T(8,128)}), f32[1,1,512,4,128]{4,2,3,1,0:T(8,128)}) %reduce-scatter.3.cloned.1.call-update) | async-done | bytes 1048592 | tf_op jit(solution)/shard_map/reduce_scatter | solution.py:83
  270.1 1.3 convert_bitcast_fusion.1
  271.4 0.1 pad_maximum_fusion.2
  271.6 1.6 copy.51
  (33 shorter events, 1.1 us)
Async XLA Ops:
  7.2 19.9 %copy-start = (bf16[1,1,512,8,128]{4,3,2,1,0:T(8,128)(2,1)S(1)}, bf16[1,1,512,8,128]{4,3,2,1,0:T(8,128)(2,1)}, u32[]{:S(2)}) copy-start(bf16[1,1,512,8,128]{4,3,2,1,0:T(8,128)(2,1)} %param.7) | copy-start | bytes 3145732
  7.2 22.1 %copy-start.1 = (bf16[1,1,512,8,128]{4,3,2,1,0:T(8,128)(2,1)S(1)}, bf16[1,1,512,8,128]{4,3,2,1,0:T(8,128)(2,1)}, u32[]{:S(2)}) copy-start(bf16[1,1,512,8,128]{4,3,2,1,0:T(8,128)(2,1)} %param.4) | copy-start | bytes 3145732
  7.2 58.8 %all-gather.3.cloned.1.call-start = ((), (), s32[]{:S(2)}) async-start(), calls=%async_computation.2 | async-start | bytes 2621440 | tf_op jit(solution)/shard_map/all_gather | solution.py:75
  17.1 95.6 %all-gather.5.cloned.1.call-start = ((), (), s32[]{:S(2)}) async-start(), calls=%async_computation.3 | async-start | bytes 2621440 | tf_op jit(solution)/shard_map/all_gather | solution.py:76
  27.0 163.6 %reduce-scatter.5.cloned.1.call-start = ((), (), s32[]{:S(2)}) async-start(), calls=%async_computation.5 | async-start | bytes 5242880 | tf_op jit(solution)/shard_map/reduce_scatter | solution.py:84
  76.6 193.5 %reduce-scatter.3.cloned.1.call-start = ((), (), s32[]{:S(2)}) async-start(), calls=%async_computation.4 | async-start | bytes 5242880 | tf_op jit(solution)/shard_map/reduce_scatter | solution.py:83
  130.8 2.2 copy-start.2
  163.2 2.7 copy-start.3
  173.9 1.9 copy-start.5
  191.9 79.6 %copy-start.4 = (bf16[1,1,512,4,1,128]{5,2,3,4,1,0:T(8,128)(2,1)S(1)}, bf16[1,1,512,4,1,128]{5,2,3,4,1,0:T(8,128)(2,1)}, u32[]{:S(2)}) copy-start(bf16[1,1,512,4,1,128]{5,2,3,4,1,0:T(8,128)(2,1)} %fusion.11) | copy-start | bytes 1572868
Sparse Core Ops, SparseCore 0:
  17.3 48.6 all-gather.2
  68.1 44.6 all-gather.4
  115.1 75.4 reduce-scatter.4
  192.8 77.2 reduce-scatter.2
where the time goes:
time: 282 us; the launch traced here: 280 us
  waiting for transfers between devices  160 us (57%)
  local copies, waits for them, and re-layouts  65.7 us (23%)
  matrix products  28.3 us (10%)
  between operations  14.1 us (5%)
  other arithmetic  11.9 us (4%)
    reduce_scatter x1, waiting for transfers between devices, per_device(): lax.psum_scatter(col_local[2], 'ctx', scatter_dimension=1, tiled=True)  76.4 us
    all_gather x1, waiting for transfers between devices, per_device(): lax.all_gather(col_parts[2], 'ctx', axis=1, tiled=True)  35.9 us
    all_gather x1, waiting for transfers between devices, per_device(): lax.all_gather(col_parts[1], 'ctx', axis=1, tiled=True)  34.3 us
    slice x4, local copies, waits for them, and re-layouts, per_device(): row_parts = tuple((array[:, :, :, 0::2] for array in arrays))  26.8 us
    slice x4, local copies, waits for them, and re-layouts, per_device(): col_parts = tuple((array[:, :, :, 1::2] for array in arrays))  22.3 us
    reduce_scatter x1, waiting for transfers between devices, per_device(): lax.psum_scatter(col_local[3], 'ctx', scatter_dimension=1, tiled=True)  12.9 us
    unnamed x18, local copies, waits for them, and re-layouts  8.35 us
    dot_general x2, matrix products, attend(): jnp.einsum(layout + ',' + key_form + '->bxhqk', query_in, key_in, preferr...  6.97 us
  transfers between devices with their start and end apart: 4, of which 4 were waited for; matrix products, arithmetic and copies ran while one was open for 33% of the time, Pallas kernels for 0%

commit v1 on v0

--- a/solution.py
+++ b/solution.py
@@ -1,9 +1,351 @@
+import functools
 import math
 
 import jax
 import jax.numpy as jnp
 from jax import lax
+from jax.experimental import pallas as pl
+from jax.experimental.pallas import tpu as pltpu
 from jax.sharding import PartitionSpec as P
+
+MESH = pl.DeviceIdType.MESH
+F32 = jnp.float32
+BF16 = jnp.bfloat16
+NT = (((1,), (1,)), ((), ()))
+NN = (((1,), (0,)), ((), ()))
+TN = (((0,), (0,)), ((), ()))
+
+
+def mm(a, b, dims):
+    return lax.dot_general(a, b, dims, preferred_element_type=F32)
+
+
+def row_head(buf, stage, i, tokens, depth):
+    scaling = 1.0 / math.sqrt(depth)
+    block = tokens // 2
+    keys = buf[i, 1]
+    values = buf[i, 2]
+    parts = []
+    for b in (1, 0):
+        rows = pl.ds(b * block, block)
+        span = (b + 1) * block
+        q = buf[i, 0, rows]
+        g = buf[i, 3, rows]
+        k = keys[:span]
+        v = values[:span]
+        s = mm(q, k, NT) * scaling
+        qpos = lax.broadcasted_iota(jnp.int32, (block, span), 0) + b * block
+        kpos = lax.broadcasted_iota(jnp.int32, (block, span), 1)
+        s = jnp.where(kpos <= qpos, s, -1e30)
+        top = jnp.max(s, axis=-1, keepdims=True)
+        e = jnp.exp(s - top)
+        p = e * (1.0 / jnp.sum(e, axis=-1, keepdims=True))
+        pb = p.astype(BF16)
+        o = mm(pb, v, NN).astype(BF16).astype(F32)
+        dots = jnp.sum(g.astype(F32) * o, axis=-1, keepdims=True)
+        dp = mm(g, v, NT)
+        ds = (p * (dp - dots) * scaling).astype(BF16)
+        stage[0, 2 * i, rows] = o
+        stage[1, 2 * i, rows] = mm(ds, k, NN)
+        dk = mm(ds, q, TN)
+        dv = mm(pb, g, TN)
+        if b == 1:
+            stage[2, 2 * i] = dk
+            stage[3, 2 * i] = dv
+        else:
+            stage[2, 2 * i, pl.ds(0, span)] += dk
+            stage[3, 2 * i, pl.ds(0, span)] += dv
+
+
+def column_block(queries, keys, scaling):
+    outs = []
+    grads = [None] * len(keys)
+    for q, g, seen in queries:
+        s = [jnp.sum(q * k, axis=-1, keepdims=True) * scaling for k, _ in keys[:seen]]
+        dp = [jnp.sum(g * v, axis=-1, keepdims=True) for _, v in keys[:seen]]
+        top = functools.reduce(jnp.maximum, s)
+        e = [jnp.exp(x - top) for x in s]
+        inverse = 1.0 / functools.reduce(jnp.add, e)
+        p = [x * inverse for x in e]
+        dots = functools.reduce(jnp.add, [x * y for x, y in zip(p, dp)])
+        ds = [x * (y - dots) * scaling for x, y in zip(p, dp)]
+        o = functools.reduce(jnp.add, [x * kv[1] for x, kv in zip(p, keys)])
+        dq = functools.reduce(jnp.add, [x * kv[0] for x, kv in zip(ds, keys)])
+        outs.append((o, dq))
+        for j in range(seen):
+            dk, dv = ds[j] * q, p[j] * g
+            grads[j] = (dk, dv) if grads[j] is None else (grads[j][0] + dk, grads[j][1] + dv)
+    return outs, grads
+
+
+def kernel(
+    q_ref, k_ref, v_ref, g_ref, o_out, dq_out, dk_out, dv_out,
+    wide, rows_in, cols_in, stage, in_a, in_b, in_c, ret_a, ret_b, ret_c,
+    sent1, got_a, got_b, got_c, sent2, back_a, back_b, back_c,
+):
+    tokens, local_heads, depth = q_ref.shape
+    heads = local_heads // 2
+    scaling = 1.0 / math.sqrt(depth)
+    me = lax.axis_index("ctx")
+    barrier = pltpu.get_barrier_semaphore()
+    for step in range(1, 4):
+        pl.semaphore_signal(
+            barrier, inc=1, device_id={"ctx": lax.rem(me + step, 4)}, device_id_type=MESH
+        )
+
+    def remote(src, dst, send, recv, target):
+        return pltpu.make_async_remote_copy(
+            src_ref=src, dst_ref=dst, send_sem=send, recv_sem=recv,
+            device_id={"ctx": target}, device_id_type=MESH,
+        )
+
+    def kv_to(i, target, buf, got, slot):
+        return remote(cols_in.at[i, pl.ds(1, 2)], buf.at[i], sent1.at[slot, i], got.at[i], target)
+
+    def all_to(i):
+        return remote(cols_in.at[i], in_c.at[i], sent1.at[0, i], got_c.at[i], 2)
+
+    CH = 64
+    chunks = tokens // CH
+
+    def split(ref, at):
+        def widen(c, _):
+            x = ref[pl.ds(c * CH, CH)].astype(F32)
+            wide[pl.ds(c * CH * local_heads, CH * local_heads)] = x.reshape(CH * local_heads, depth)
+            return 0
+
+        lax.fori_loop(0, chunks, widen, 0)
+
+        def pick(c, _):
+            for h in range(local_heads):
+                x = wide[pl.ds(c * CH * local_heads + h, CH, stride=local_heads)].astype(BF16)
+                buf = rows_in if h % 2 == 0 else cols_in
+                buf[h // 2, at, pl.ds(c * CH, CH)] = x
+            return 0
+
+        lax.fori_loop(0, chunks, pick, 0)
+
+    split(k_ref, 1)
+    split(v_ref, 2)
+    pl.semaphore_wait(barrier, 3)
+
+    def each(count, body):
+        def step(i, _):
+            body(i)
+            return 0
+
+        lax.fori_loop(0, count, step, 0)
+
+    @pl.when(me == 0)
+    def _():
+        def go(i):
+            kv_to(i, 2, in_a, got_a, 0).start()
+            kv_to(i, 1, in_a, got_a, 1).start()
+
+        each(heads, go)
+
+    @pl.when(me == 1)
+    def _():
+        each(heads, lambda i: kv_to(i, 2, in_b, got_b, 0).start())
+
+    split(q_ref, 0)
+    split(g_ref, 3)
+
+    @pl.when(me == 3)
+    def _():
+        each(heads, lambda i: all_to(i).start())
+
+    def ret_a_copy(i, src, target, slot):
+        return remote(src.at[i], ret_a.at[i], sent2.at[slot, i], back_a.at[i], target)
+
+    def ret_b_copy(i):
+        return remote(in_a.at[i], ret_b.at[i], sent2.at[0, i], back_b.at[i], 0)
+
+    def ret_c_copy(i):
+        return remote(in_c.at[i], ret_c.at[i], sent2.at[2, i], back_c.at[i], 3)
+
+    CB = 128
+
+    def own(i, rows):
+        return [cols_in[i, a, rows].astype(F32) for a in range(4)]
+
+    def put_own(i, rows, out, grad):
+        stage[0, 2 * i + 1, rows] = out[0]
+        stage[1, 2 * i + 1, rows] = out[1]
+        stage[2, 2 * i + 1, rows] = grad[0]
+        stage[3, 2 * i + 1, rows] = grad[1]
+
+    def pair(buf, i, rows):
+        return (buf[i, 0, rows].astype(F32), buf[i, 1, rows].astype(F32))
+
+    def put_pair(buf, i, rows, grad):
+        buf[i, 0, rows] = grad[0].astype(BF16)
+        buf[i, 1, rows] = grad[1].astype(BF16)
+
+    def body(i):
+        row_head(rows_in, stage, i, tokens, depth)
+
+        @pl.when(me == 0)
+        def _():
+            def block(c):
+                rows = pl.ds(c * CB, CB)
+                q, k, v, g = own(i, rows)
+                outs, grads = column_block([(q, g, 1)], [(k, v)], scaling)
+                put_own(i, rows, outs[0], grads[0])
+
+            each(tokens // CB, block)
+
+        @pl.when(me == 1)
+        def _():
+            kv_to(i, 1, in_a, got_a, 1).wait_recv()
+
+            def block(c):
+                rows = pl.ds(c * CB, CB)
+                q, k, v, g = own(i, rows)
+                outs, grads = column_block([(q, g, 2)], [pair(in_a, i, rows), (k, v)], scaling)
+                put_own(i, rows, outs[0], grads[1])
+                put_pair(in_a, i, rows, grads[0])
+
+            each(tokens // CB, block)
+            ret_a_copy(i, in_a, 0, 0).start()
+
+        @pl.when(me == 2)
+        def _():
+            kv_to(i, 2, in_a, got_a, 0).wait_recv()
+            kv_to(i, 2, in_b, got_b, 0).wait_recv()
+            all_to(i).wait_recv()
+
+            def block(c):
+                rows = pl.ds(c * CB, CB)
+                q, k, v, g = own(i, rows)
+                q3, k3, v3, g3 = [in_c[i, a, rows].astype(F32) for a in range(4)]
+                outs, grads = column_block(
+                    [(q, g, 3), (q3, g3, 4)],
+                    [pair(in_a, i, rows), pair(in_b, i, rows), (k, v), (k3, v3)],
+                    scaling,
+                )
+                put_own(i, rows, outs[0], grads[2])
+                put_pair(in_a, i, rows, grads[0])
+                put_pair(in_b, i, rows, grads[1])
+                for a, x in enumerate(outs[1] + grads[3]):
+                    in_c[i, a, rows] = x.astype(BF16)
+
+            each(tokens // CB, block)
+            ret_b_copy(i).start()
+            ret_a_copy(i, in_b, 1, 1).start()
+            ret_c_copy(i).start()
+
+    each(heads, body)
+
+    def join(at, ref):
+        def spread(c):
+            for h in range(local_heads):
+                wide[pl.ds(c * CH * local_heads + h, CH, stride=local_heads)] = stage[
+                    at, h, pl.ds(c * CH, CH)
+                ]
+
+        each(chunks, spread)
+
+        def narrow(c):
+            x = wide[pl.ds(c * CH * local_heads, CH * local_heads)]
+            ref[pl.ds(c * CH, CH)] = x.reshape(CH, local_heads, depth).astype(BF16)
+
+        each(chunks, narrow)
+
+    def add(i, at, x):
+        stage[at, 2 * i + 1] += x.astype(F32)
+
+    @pl.when(me == 3)
+    def _():
+        def take(i):
+            ret_c_copy(i).wait_recv()
+            for a in range(4):
+                stage[a, 2 * i + 1] = ret_c[i, a].astype(F32)
+
+        each(heads, take)
+
+    join(0, o_out)
+    join(1, dq_out)
+
+    @pl.when(me == 0)
+    def _():
+        def take(i):
+            ret_a_copy(i, in_a, 0, 0).wait_recv()
+            ret_b_copy(i).wait_recv()
+            for a in range(2):
+                add(i, 2 + a, ret_a[i, a].astype(F32) + ret_b[i, a].astype(F32))
+
+        each(heads, take)
+
+    @pl.when(me == 1)
+    def _():
+        def take(i):
+            ret_a_copy(i, in_b, 1, 1).wait_recv()
+            for a in range(2):
+                add(i, 2 + a, ret_a[i, a])
+
+        each(heads, take)
+
+    join(2, dk_out)
+    join(3, dv_out)
+
+    @pl.when(me == 0)
+    def _():
+        def done(i):
+            kv_to(i, 2, in_a, got_a, 0).wait_send()
+            kv_to(i, 1, in_a, got_a, 1).wait_send()
+
+        each(heads, done)
+
+    @pl.when(me == 1)
+    def _():
+        def done(i):
+            kv_to(i, 2, in_b, got_b, 0).wait_send()
+            ret_a_copy(i, in_a, 0, 0).wait_send()
+
+        each(heads, done)
+
+    @pl.when(me == 2)
+    def _():
+        def done(i):
+            ret_b_copy(i).wait_send()
+            ret_a_copy(i, in_b, 1, 1).wait_send()
+            ret_c_copy(i).wait_send()
+
+        each(heads, done)
+
+    @pl.when(me == 3)
+    def _():
+        each(heads, lambda i: all_to(i).wait_send())
+
+
+def fused(queries, key_vecs, value_vecs, grad_out):
+    shape = queries.shape
+    tokens, local_heads, depth = shape[2:]
+    heads = local_heads // 2
+    flat = [x.reshape(tokens, local_heads, depth) for x in (queries, key_vecs, value_vecs, grad_out)]
+    vmem = pl.BlockSpec(memory_space=pltpu.VMEM)
+    two = pltpu.VMEM((heads, 2, tokens, depth), BF16)
+    four = pltpu.VMEM((heads, 4, tokens, depth), BF16)
+    dma = pltpu.SemaphoreType.DMA
+    results = pl.pallas_call(
+        kernel,
+        out_shape=[jax.ShapeDtypeStruct((tokens, local_heads, depth), BF16)] * 4,
+        in_specs=[vmem] * 4,
+        out_specs=[vmem] * 4,
+        scratch_shapes=[
+            pltpu.VMEM((tokens * local_heads, depth), F32),
+            four, four,
+            pltpu.VMEM((4, local_heads, tokens, depth), F32),
+            two, two, four, two, two, four,
+            dma((2, heads)), dma((heads,)), dma((heads,)), dma((heads,)),
+            dma((3, heads)), dma((heads,)), dma((heads,)), dma((heads,)),
+        ],
+        compiler_params=pltpu.CompilerParams(
+            collective_id=0, has_side_effects=True, vmem_limit_bytes=56 * 1024 * 1024
+        ),
+    )(*flat)
+    return tuple(x.reshape(shape) for x in results)
 
 
 def causal(length):
@@ -98,6 +440,7 @@
 
 
 def solution(mesh):
+    body = fused if mesh.shape["ctx"] == 4 else per_device
     placed = (
         P(("groups", "dp"), "ctx", None, "head", None),
         P(("groups", "dp"), "ctx", None, "head", None),
@@ -105,7 +448,7 @@
         P(("groups", "dp"), "ctx", None, "head", None),
     )
     return jax.shard_map(
-        per_device,
+        body,
         mesh=mesh,
         in_specs=placed,
         out_specs=(

time: 282 us -> 77.7 us (0.28)
  waiting for transfers between devices: 160 us -> 0 us
  Pallas kernels: 0 us -> 70.3 us
  local copies, waits for them, and re-layouts: 65.7 us -> 6.53 us
  matrix products: 28.3 us -> 0 us
  between operations: 14.1 us -> 0.65 us
  other arithmetic: 11.9 us -> 0 us
    reduce_scatter x2 -> x0, waiting for transfers between devices: 89.3 us -> none  [the longest x1 76.4 us: per_device(): lax.psum_scatter(col_local[2], 'ctx', scatter_dimension=1, tiled=True)]
    pallas_call x0 -> x1, Pallas kernels: none -> 70.3 us  [fused(): pl.pallas_call(kernel, out_shape=[jax.ShapeDtypeStruct((tokens, local_hea...]
    all_gather x2 -> x0, waiting for transfers between devices: 70.2 us -> none  [the longest x1 35.9 us: per_device(): lax.all_gather(col_parts[2], 'ctx', axis=1, tiled=True)]
    slice x8 -> x0, local copies, waits for them, and re-layouts: 49.1 us -> none  [the longest x4 26.8 us: per_device(): row_parts = tuple((array[:, :, :, 0::2] for array in arrays))]
    dot_general x10 -> x0, matrix products: 28.3 us -> none  [the longest x2 6.97 us: attend(): jnp.einsum(layout + ',' + key_form + '->bxhqk', query_in, key_in, preferr...]
    transpose x2 -> x0, other arithmetic: 6.25 us -> none  [the longest x1 3.13 us: attend(): jnp.einsum('bxhqk,' + layout + '->' + key_form, dscores, query_in, prefer...]
    dot_general x4 -> x0, local copies, waits for them, and re-layouts: 4.76 us -> none  [the longest x1 2.32 us: attend(): jnp.einsum(layout + ',' + key_form + '->bxhqk', grad_in, value_in, prefer...]
    another operation x9 -> x0, other arithmetic: 3.29 us -> none  [the longest x6 2.98 us: merge_heads(): stacked = jnp.stack((first_part, second_part), axis=4)]
  transfers between devices with their start and end apart: 4 -> 0, of which waited for: 4 -> 0; matrix products, arithmetic and copies ran while one was open for 33% -> 0% of each run, Pallas kernels for 0% -> 0%
where the time goes in v1:
time: 77.7 us; the launch traced here: 77.5 us
  Pallas kernels  70.3 us (90%)
  local copies, waits for them, and re-layouts  6.53 us (8%)
    pallas_call x1, Pallas kernels, fused(): pl.pallas_call(kernel, out_shape=[jax.ShapeDtypeStruct((tokens, local_hea...  70.3 us
    unnamed x10, local copies, waits for them, and re-layouts  6.53 us

profile of v1, /device:TPU:0, one launch (start us, length us, event | category | flops | bytes accessed | tf_op | source)
XLA Modules:
  0.0 77.5 jit_solution(11922077213651697032)
XLA Ops:
  0.6 70.3 %shard_map.75 = (bf16[512,8,128]{2,1,0:T(8,128)(2,1)}, bf16[512,8,128]{2,1,0:T(8,128)(2,1)}, bf16[512,8,128]{2,1,0:T(8,128)(2,1)}, bf16[512,8,128]{2,1,0:T(8,128)(2,1)}) custom-call(bf16[512,8,128]{2,1,0:T(8,128)(2,1)} %bitcast.12, bf16[512,8,128]{2,1,0:T(8,128)(2,1)} %bitcast.13, bf16[512,8,128]{2,1,0:T(8,128)(2,1)} %bitcast.14, bf16[512,8,128]{2,1,0:T(8,128)(2,1)} %bitcast.15), custom_call_target="tpu_custom_call" | custom-call | tf_op jit(solution)/shard_map/pallas_call | solution.py:331
  71.0 0.0 copy-start.2
  71.0 2.4 %copy.12 = bf16[1,1,512,8,128]{4,3,2,1,0:T(8,128)(2,1)} copy(bf16[1,1,512,8,128]{4,3,2,1,0:T(8,128)(2,1)} %bitcast.11) | data formatting | bytes 2097152
  73.3 0.0 copy-done.2
  73.3 0.0 copy-start.1
  73.3 1.0 %copy.13 = bf16[1,1,512,8,128]{4,3,2,1,0:T(8,128)(2,1)} copy(bf16[1,1,512,8,128]{4,3,2,1,0:T(8,128)(2,1)S(1)} %bitcast.10) | data formatting | bytes 2097152
  74.3 0.6 copy-done.1
  74.9 0.0 copy-start
  74.9 1.0 %copy.14 = bf16[1,1,512,8,128]{4,3,2,1,0:T(8,128)(2,1)} copy(bf16[1,1,512,8,128]{4,3,2,1,0:T(8,128)(2,1)S(1)} %bitcast.9) | data formatting | bytes 2097152
  75.9 0.6 copy-done
  76.5 1.0 %copy.15 = bf16[1,1,512,8,128]{4,3,2,1,0:T(8,128)(2,1)} copy(bf16[1,1,512,8,128]{4,3,2,1,0:T(8,128)(2,1)S(1)} %bitcast.8) | data formatting | bytes 2097152
Async XLA Ops:
  71.0 2.4 %copy-start.2 = (bf16[512,8,128]{2,1,0:T(8,128)(2,1)S(1)}, bf16[512,8,128]{2,1,0:T(8,128)(2,1)}, u32[]{:S(2)}) copy-start(bf16[512,8,128]{2,1,0:T(8,128)(2,1)} %get-tuple-element.9) | copy-start | bytes 3145732
  73.3 1.6 %copy-start.1 = (bf16[512,8,128]{2,1,0:T(8,128)(2,1)S(1)}, bf16[512,8,128]{2,1,0:T(8,128)(2,1)}, u32[]{:S(2)}) copy-start(bf16[512,8,128]{2,1,0:T(8,128)(2,1)} %get-tuple-element.10) | copy-start | bytes 3145732
  74.9 1.6 %copy-start = (bf16[512,8,128]{2,1,0:T(8,128)(2,1)S(1)}, bf16[512,8,128]{2,1,0:T(8,128)(2,1)}, u32[]{:S(2)}) copy-start(bf16[512,8,128]{2,1,0:T(8,128)(2,1)} %get-tuple-element.11) | copy-start | bytes 3145732

commit v2 on v0

--- a/solution.py
+++ b/solution.py
@@ -1,9 +1,369 @@
+import functools
 import math
 
 import jax
 import jax.numpy as jnp
 from jax import lax
+from jax.experimental import pallas as pl
+from jax.experimental.pallas import tpu as pltpu
 from jax.sharding import PartitionSpec as P
+
+MESH = pl.DeviceIdType.MESH
+F32 = jnp.float32
+BF16 = jnp.bfloat16
+NT = (((1,), (1,)), ((), ()))
+NN = (((1,), (0,)), ((), ()))
+TN = (((0,), (0,)), ((), ()))
+
+
+def mm(a, b, dims):
+    return lax.dot_general(a, b, dims, preferred_element_type=F32)
+
+
+def row_piece(buf, acc, stage, i, b, tokens, depth):
+    scaling = 1.0 / math.sqrt(depth)
+    block = tokens // 2
+    rows = pl.ds(b * block, block)
+    span = (b + 1) * block
+    q = buf[i, 0, rows]
+    g = buf[i, 3, rows]
+    k = buf[i, 1, pl.ds(0, span)]
+    v = buf[i, 2, pl.ds(0, span)]
+    s = mm(q, k, NT) * scaling
+    qpos = lax.broadcasted_iota(jnp.int32, (block, span), 0) + b * block
+    kpos = lax.broadcasted_iota(jnp.int32, (block, span), 1)
+    s = jnp.where(kpos <= qpos, s, -1e30)
+    top = jnp.max(s, axis=-1, keepdims=True)
+    e = jnp.exp(s - top)
+    p = e * (1.0 / jnp.sum(e, axis=-1, keepdims=True))
+    pb = p.astype(BF16)
+    o = mm(pb, v, NN).astype(BF16)
+    dots = jnp.sum(g.astype(F32) * o.astype(F32), axis=-1, keepdims=True)
+    dp = mm(g, v, NT)
+    ds = (p * (dp - dots) * scaling).astype(BF16)
+    stage[i, 0, rows] = o
+    stage[i, 1, rows] = mm(ds, k, NN).astype(BF16)
+    dk = mm(ds, q, TN)
+    dv = mm(pb, g, TN)
+    if b == 1:
+        acc[0] = dk[:block]
+        acc[1] = dv[:block]
+        stage[i, 2, rows] = dk[block:].astype(BF16)
+        stage[i, 3, rows] = dv[block:].astype(BF16)
+    else:
+        stage[i, 2, rows] = (acc[0] + dk).astype(BF16)
+        stage[i, 3, rows] = (acc[1] + dv).astype(BF16)
+
+
+def column_block(queries, keys, scaling):
+    outs = []
+    grads = [None] * len(keys)
+    for q, g, seen in queries:
+        s = [jnp.sum(q * k, axis=-1, keepdims=True) * scaling for k, _ in keys[:seen]]
+        dp = [jnp.sum(g * v, axis=-1, keepdims=True) for _, v in keys[:seen]]
+        top = functools.reduce(jnp.maximum, s)
+        e = [jnp.exp(x - top) for x in s]
+        inverse = 1.0 / functools.reduce(jnp.add, e)
+        p = [x * inverse for x in e]
+        dots = functools.reduce(jnp.add, [x * y for x, y in zip(p, dp)])
+        ds = [x * (y - dots) * scaling for x, y in zip(p, dp)]
+        o = functools.reduce(jnp.add, [x * kv[1] for x, kv in zip(p, keys)])
+        dq = functools.reduce(jnp.add, [x * kv[0] for x, kv in zip(ds, keys)])
+        outs.append((o, dq))
+        for j in range(seen):
+            dk, dv = ds[j] * q, p[j] * g
+            grads[j] = (dk, dv) if grads[j] is None else (grads[j][0] + dk, grads[j][1] + dv)
+    return outs, grads
+
+
+QUARTERS = 4
+
+
+def each(count, body):
+    def step(i, _):
+        body(i)
+        return 0
+
+    lax.fori_loop(0, count, step, 0)
+
+
+def kernel(
+    q_ref, k_ref, v_ref, g_ref, rows_out, cols_out,
+    fetched, wide, rows_in, cols_in, rows_stage, cols_stage, acc, own_grads,
+    in_a, in_b, in_c, ret_a, ret_b, ret_c,
+    load, sent1, got_a, got_b, got_c, sent2, back_a, back_b, back_c, left_rows, left_cols,
+):
+    tokens, local_heads, depth = q_ref.shape
+    heads = local_heads // 2
+    columns = tokens // QUARTERS
+    chunks = heads * QUARTERS
+    scaling = 1.0 / math.sqrt(depth)
+    me = lax.axis_index("ctx")
+    refs = (q_ref, k_ref, v_ref, g_ref)
+
+    def fetch(at, quarter):
+        part = pl.ds(quarter * columns, columns)
+        return pltpu.make_async_copy(
+            refs[at].at[part], fetched.at[at, part], load.at[at, quarter]
+        )
+
+    for quarter in range(QUARTERS):
+        for at in (1, 2, 0, 3):
+            fetch(at, quarter).start()
+
+    barrier = pltpu.get_barrier_semaphore()
+    for step in range(1, 4):
+        pl.semaphore_signal(
+            barrier, inc=1, device_id={"ctx": lax.rem(me + step, 4)}, device_id_type=MESH
+        )
+
+    def remote(src, dst, send, recv, target):
+        return pltpu.make_async_remote_copy(
+            src_ref=src, dst_ref=dst, send_sem=send, recv_sem=recv,
+            device_id={"ctx": target}, device_id_type=MESH,
+        )
+
+    def kv_to(c, target, buf, got, slot):
+        return remote(cols_in.at[c, pl.ds(1, 2)], buf.at[c], sent1.at[slot, c], got.at[c], target)
+
+    def all_to(c):
+        return remote(cols_in.at[c], in_c.at[c], sent1.at[0, c], got_c.at[c], 2)
+
+    def split(at, quarter):
+        fetch(at, quarter).wait()
+        x = fetched[at, pl.ds(quarter * columns, columns)].astype(F32)
+        wide[at] = x.reshape(columns * local_heads, depth)
+        for h in range(local_heads):
+            x = wide[at, pl.ds(h, columns, stride=local_heads)].astype(BF16)
+            if h % 2 == 0:
+                rows_in[h // 2, at, pl.ds(quarter * columns, columns)] = x
+            else:
+                cols_in[quarter * heads + h // 2, at] = x
+
+    pl.semaphore_wait(barrier, 3)
+
+    def prepare(quarter):
+        split(1, quarter)
+        split(2, quarter)
+
+        @pl.when(me == 0)
+        def _():
+            def go(i):
+                kv_to(quarter * heads + i, 2, in_a, got_a, 0).start()
+                kv_to(quarter * heads + i, 1, in_a, got_a, 1).start()
+
+            each(heads, go)
+
+        @pl.when(me == 1)
+        def _():
+            each(heads, lambda i: kv_to(quarter * heads + i, 2, in_b, got_b, 0).start())
+
+        split(0, quarter)
+        split(3, quarter)
+
+        @pl.when(me == 3)
+        def _():
+            each(heads, lambda i: all_to(quarter * heads + i).start())
+
+    each(QUARTERS, prepare)
+
+    def ret_a_copy(c, src, target, slot):
+        return remote(src.at[c], ret_a.at[c], sent2.at[slot, c], back_a.at[c], target)
+
+    def ret_b_copy(c):
+        return remote(in_a.at[c], ret_b.at[c], sent2.at[0, c], back_b.at[c], 0)
+
+    def ret_c_copy(c):
+        return remote(in_c.at[c], ret_c.at[c], sent2.at[2, c], back_c.at[c], 3)
+
+    def rows_leave(i):
+        return pltpu.make_async_copy(rows_stage.at[i], rows_out.at[i], left_rows.at[i])
+
+    def cols_leave(c):
+        return pltpu.make_async_copy(cols_stage.at[c], cols_out.at[c], left_cols.at[c])
+
+    def own(c):
+        return [cols_in[c, a].astype(F32) for a in range(4)]
+
+    def put(ref, c, first, values):
+        for a, x in enumerate(values):
+            ref[c, first + a] = x.astype(ref.dtype)
+
+    def pair(buf, c):
+        return (buf[c, 0].astype(F32), buf[c, 1].astype(F32))
+
+    def body(c):
+        @pl.when(c % QUARTERS == 0)
+        def _():
+            row_piece(rows_in, acc, rows_stage, c // QUARTERS, 1, tokens, depth)
+
+        @pl.when(c % QUARTERS == 2)
+        def _():
+            row_piece(rows_in, acc, rows_stage, c // QUARTERS, 0, tokens, depth)
+            rows_leave(c // QUARTERS).start()
+
+        @pl.when(me == 0)
+        def _():
+            q, k, v, g = own(c)
+            outs, grads = column_block([(q, g, 1)], [(k, v)], scaling)
+            put(cols_stage, c, 0, outs[0])
+            put(own_grads, c, 0, grads[0])
+
+        @pl.when(me == 1)
+        def _():
+            kv_to(c, 1, in_a, got_a, 1).wait_recv()
+            q, k, v, g = own(c)
+            outs, grads = column_block([(q, g, 2)], [pair(in_a, c), (k, v)], scaling)
+            put(in_a, c, 0, grads[0])
+            ret_a_copy(c, in_a, 0, 0).start()
+            put(cols_stage, c, 0, outs[0])
+            put(own_grads, c, 0, grads[1])
+
+        @pl.when(me == 2)
+        def _():
+            kv_to(c, 2, in_a, got_a, 0).wait_recv()
+            kv_to(c, 2, in_b, got_b, 0).wait_recv()
+            all_to(c).wait_recv()
+            q, k, v, g = own(c)
+            q3, k3, v3, g3 = [in_c[c, a].astype(F32) for a in range(4)]
+            outs, grads = column_block(
+                [(q, g, 3), (q3, g3, 4)],
+                [pair(in_a, c), pair(in_b, c), (k, v), (k3, v3)],
+                scaling,
+            )
+            put(in_a, c, 0, grads[0])
+            put(in_b, c, 0, grads[1])
+            put(in_c, c, 0, outs[1] + grads[3])
+            ret_b_copy(c).start()
+            ret_a_copy(c, in_b, 1, 1).start()
+            ret_c_copy(c).start()
+            put(cols_stage, c, 0, outs[0] + grads[2])
+            cols_leave(c).start()
+
+    each(chunks, body)
+
+    @pl.when(me == 0)
+    def _():
+        def take(c):
+            ret_a_copy(c, in_a, 0, 0).wait_recv()
+            ret_b_copy(c).wait_recv()
+            total = [
+                own_grads[c, a] + ret_a[c, a].astype(F32) + ret_b[c, a].astype(F32)
+                for a in range(2)
+            ]
+            put(cols_stage, c, 2, total)
+            cols_leave(c).start()
+
+        each(chunks, take)
+
+    @pl.when(me == 1)
+    def _():
+        def take(c):
+            ret_a_copy(c, in_b, 1, 1).wait_recv()
+            put(cols_stage, c, 2, [own_grads[c, a] + ret_a[c, a].astype(F32) for a in range(2)])
+            cols_leave(c).start()
+
+        each(chunks, take)
+
+    @pl.when(me == 3)
+    def _():
+        def take(c):
+            ret_c_copy(c).wait_recv()
+            cols_stage[c] = ret_c[c]
+            cols_leave(c).start()
+
+        each(chunks, take)
+
+    each(heads, lambda i: rows_leave(i).wait())
+    each(chunks, lambda c: cols_leave(c).wait())
+
+    @pl.when(me == 0)
+    def _():
+        def done(c):
+            kv_to(c, 2, in_a, got_a, 0).wait_send()
+            kv_to(c, 1, in_a, got_a, 1).wait_send()
+
+        each(chunks, done)
+
+    @pl.when(me == 1)
+    def _():
+        def done(c):
+            kv_to(c, 2, in_b, got_b, 0).wait_send()
+            ret_a_copy(c, in_a, 0, 0).wait_send()
+
+        each(chunks, done)
+
+    @pl.when(me == 2)
+    def _():
+        def done(c):
+            ret_b_copy(c).wait_send()
+            ret_a_copy(c, in_b, 1, 1).wait_send()
+            ret_c_copy(c).wait_send()
+
+        each(chunks, done)
+
+    @pl.when(me == 3)
+    def _():
+        each(chunks, lambda c: all_to(c).wait_send())
+
+
+def join_kernel(rows_ref, cols_ref, o_out, dq_out, dk_out, dv_out, wide):
+    columns, local_heads, depth = o_out.shape
+    for a, out in enumerate((o_out, dq_out, dk_out, dv_out)):
+        for h in range(local_heads):
+            x = rows_ref[h // 2, a] if h % 2 == 0 else cols_ref[h // 2, a]
+            wide[a, pl.ds(h, columns, stride=local_heads)] = x.astype(F32)
+        out[...] = wide[a].reshape(columns, local_heads, depth).astype(BF16)
+
+
+def fused(queries, key_vecs, value_vecs, grad_out):
+    shape = queries.shape
+    tokens, local_heads, depth = shape[2:]
+    heads = local_heads // 2
+    columns = tokens // QUARTERS
+    chunks = heads * QUARTERS
+    flat = [x.reshape(tokens, local_heads, depth) for x in (queries, key_vecs, value_vecs, grad_out)]
+    anywhere = pl.BlockSpec(memory_space=pl.ANY)
+    two = pltpu.VMEM((chunks, 2, columns, depth), BF16)
+    four = pltpu.VMEM((chunks, 4, columns, depth), BF16)
+    row_buf = pltpu.VMEM((heads, 4, tokens, depth), BF16)
+    dma = pltpu.SemaphoreType.DMA
+    rows, cols = pl.pallas_call(
+        kernel,
+        out_shape=[
+            jax.ShapeDtypeStruct((heads, 4, tokens, depth), BF16),
+            jax.ShapeDtypeStruct((chunks, 4, columns, depth), BF16),
+        ],
+        in_specs=[anywhere] * 4,
+        out_specs=[anywhere] * 2,
+        scratch_shapes=[
+            pltpu.VMEM((4, tokens, local_heads, depth), BF16),
+            pltpu.VMEM((4, columns * local_heads, depth), F32),
+            row_buf, four, row_buf, four,
+            pltpu.VMEM((2, tokens // 2, depth), F32),
+            pltpu.VMEM((chunks, 2, columns, depth), F32),
+            two, two, four, two, two, four,
+            dma((4, QUARTERS)),
+            dma((2, chunks)), dma((chunks,)), dma((chunks,)), dma((chunks,)),
+            dma((3, chunks)), dma((chunks,)), dma((chunks,)), dma((chunks,)),
+            dma((heads,)), dma((chunks,)),
+        ],
+        compiler_params=pltpu.CompilerParams(
+            collective_id=0, has_side_effects=True, vmem_limit_bytes=56 * 1024 * 1024
+        ),
+    )(*flat)
+    results = pl.pallas_call(
+        join_kernel,
+        grid=(QUARTERS,),
+        out_shape=[jax.ShapeDtypeStruct((tokens, local_heads, depth), BF16)] * 4,
+        in_specs=[
+            pl.BlockSpec((heads, 4, columns, depth), lambda c: (0, 0, c, 0)),
+            pl.BlockSpec((heads, 4, columns, depth), lambda c: (c, 0, 0, 0)),
+        ],
+        out_specs=[pl.BlockSpec((columns, local_heads, depth), lambda c: (c, 0, 0))] * 4,
+        scratch_shapes=[pltpu.VMEM((4, columns * local_heads, depth), F32)],
+    )(rows, cols)
+    return tuple(x.reshape(shape) for x in results)
 
 
 def causal(length):
@@ -98,6 +458,7 @@
 
 
 def solution(mesh):
+    body = fused if mesh.shape["ctx"] == 4 else per_device
     placed = (
         P(("groups", "dp"), "ctx", None, "head", None),
         P(("groups", "dp"), "ctx", None, "head", None),
@@ -105,7 +466,7 @@
         P(("groups", "dp"), "ctx", None, "head", None),
     )
     return jax.shard_map(
-        per_device,
+        body,
         mesh=mesh,
         in_specs=placed,
         out_specs=(

time: 282 us -> 66.4 us (0.24)
  waiting for transfers between devices: 160 us -> 0 us
  local copies, waits for them, and re-layouts: 65.7 us -> 0 us
  Pallas kernels: 0 us -> 65.5 us
  matrix products: 28.3 us -> 0 us
  between operations: 14.1 us -> 0.64 us
  other arithmetic: 11.9 us -> 0 us
    reduce_scatter x2 -> x0, waiting for transfers between devices: 89.3 us -> none  [the longest x1 76.4 us: per_device(): lax.psum_scatter(col_local[2], 'ctx', scatter_dimension=1, tiled=True)]
    all_gather x2 -> x0, waiting for transfers between devices: 70.2 us -> none  [the longest x1 35.9 us: per_device(): lax.all_gather(col_parts[2], 'ctx', axis=1, tiled=True)]
    pallas_call x0 -> x2, Pallas kernels: none -> 65.5 us  [the longest x1 60.1 us: fused(): pl.pallas_call(kernel, out_shape=[jax.ShapeDtypeStruct((heads, 4, tokens,...]
    slice x8 -> x0, local copies, waits for them, and re-layouts: 49.1 us -> none  [the longest x4 26.8 us: per_device(): row_parts = tuple((array[:, :, :, 0::2] for array in arrays))]
    dot_general x10 -> x0, matrix products: 28.3 us -> none  [the longest x2 6.97 us: attend(): jnp.einsum(layout + ',' + key_form + '->bxhqk', query_in, key_in, preferr...]
    unnamed x18 -> x0, local copies, waits for them, and re-layouts: 8.35 us -> none
    transpose x2 -> x0, other arithmetic: 6.25 us -> none  [the longest x1 3.13 us: attend(): jnp.einsum('bxhqk,' + layout + '->' + key_form, dscores, query_in, prefer...]
    dot_general x4 -> x0, local copies, waits for them, and re-layouts: 4.76 us -> none  [the longest x1 2.32 us: attend(): jnp.einsum(layout + ',' + key_form + '->bxhqk', grad_in, value_in, prefer...]
  transfers between devices with their start and end apart: 4 -> 0, of which waited for: 4 -> 0; matrix products, arithmetic and copies ran while one was open for 33% -> 0% of each run, Pallas kernels for 0% -> 0%
where the time goes in v2:
time: 66.4 us; the launch traced here: 66.2 us
  Pallas kernels  65.5 us (99%)
    pallas_call x1, Pallas kernels, fused(): pl.pallas_call(kernel, out_shape=[jax.ShapeDtypeStruct((heads, 4, tokens,...  60.1 us
    pallas_call x1, Pallas kernels, fused(): pl.pallas_call(join_kernel, grid=(QUARTERS,), out_shape=[jax.ShapeDtypeSt...  5.46 us

profile of v2, /device:TPU:0, one launch (start us, length us, event | category | flops | bytes accessed | tf_op | source)
XLA Modules:
  0.0 66.2 jit_solution(15590528835063034215)
XLA Ops:
  0.6 60.1 %shard_map.75 = (bf16[4,4,512,128]{3,2,1,0:T(8,128)(2,1)}, bf16[16,4,128,128]{3,2,1,0:T(8,128)(2,1)}) custom-call(bf16[512,8,128]{2,1,0:T(8,128)(2,1)} %bitcast.8, bf16[512,8,128]{2,1,0:T(8,128)(2,1)} %bitcast.9, bf16[512,8,128]{2,1,0:T(8,128)(2,1)} %bitcast.10, bf16[512,8,128]{2,1,0:T(8,128)(2,1)} %bitcast.11), custom_call_target="tpu_custom_call" | custom-call | tf_op jit(solution)/shard_map/pallas_call | solution.py:331
  60.7 5.5 %shard_map.76 = (bf16[512,8,128]{2,1,0:T(8,128)(2,1)}, bf16[512,8,128]{2,1,0:T(8,128)(2,1)}, bf16[512,8,128]{2,1,0:T(8,128)(2,1)}, bf16[512,8,128]{2,1,0:T(8,128)(2,1)}) custom-call(bf16[4,4,512,128]{3,2,1,0:T(8,128)(2,1)} %get-tuple-element.10.rows_ref, bf16[16,4,128,128]{3,2,1,0:T(8,128)(2,1)} %get-tuple-element.11.cols_ref), custom_call_target="tpu_custom_call" | custom-call | tf_op jit(solution)/shard_map/pallas_call | solution.py:355

commit v3 on v2

--- a/solution.py
+++ b/solution.py
@@ -77,6 +77,7 @@
 
 
 QUARTERS = 4
+PARTS = 1
 
 
 def each(count, body):
@@ -112,10 +113,24 @@
             fetch(at, quarter).start()
 
     barrier = pltpu.get_barrier_semaphore()
-    for step in range(1, 4):
-        pl.semaphore_signal(
-            barrier, inc=1, device_id={"ctx": lax.rem(me + step, 4)}, device_id_type=MESH
-        )
+
+    def greet(target):
+        pl.semaphore_signal(barrier, inc=1, device_id={"ctx": target}, device_id_type=MESH)
+
+    @pl.when(me < 2)
+    def _():
+        greet(1 - me)
+        greet(2)
+
+    @pl.when(me == 2)
+    def _():
+        greet(0)
+        greet(1)
+        greet(3)
+
+    @pl.when(me == 3)
+    def _():
+        greet(2)
 
     def remote(src, dst, send, recv, target):
         return pltpu.make_async_remote_copy(
@@ -140,11 +155,15 @@
             else:
                 cols_in[quarter * heads + h // 2, at] = x
 
-    pl.semaphore_wait(barrier, 3)
+    for at in (1, 2, 0, 3):
+        split(at, 0)
+    pl.semaphore_wait(barrier, jnp.where(me < 2, 2, jnp.where(me == 2, 3, 1)))
 
     def prepare(quarter):
-        split(1, quarter)
-        split(2, quarter)
+        @pl.when(quarter > 0)
+        def _():
+            split(1, quarter)
+            split(2, quarter)
 
         @pl.when(me == 0)
         def _():
@@ -158,8 +177,10 @@
         def _():
             each(heads, lambda i: kv_to(quarter * heads + i, 2, in_b, got_b, 0).start())
 
-        split(0, quarter)
-        split(3, quarter)
+        @pl.when(quarter > 0)
+        def _():
+            split(0, quarter)
+            split(3, quarter)
 
         @pl.when(me == 3)
         def _():
@@ -322,6 +343,7 @@
     heads = local_heads // 2
     columns = tokens // QUARTERS
     chunks = heads * QUARTERS
+    part = columns // PARTS
     flat = [x.reshape(tokens, local_heads, depth) for x in (queries, key_vecs, value_vecs, grad_out)]
     anywhere = pl.BlockSpec(memory_space=pl.ANY)
     two = pltpu.VMEM((chunks, 2, columns, depth), BF16)
@@ -354,14 +376,14 @@
     )(*flat)
     results = pl.pallas_call(
         join_kernel,
-        grid=(QUARTERS,),
+        grid=(QUARTERS * PARTS,),
         out_shape=[jax.ShapeDtypeStruct((tokens, local_heads, depth), BF16)] * 4,
         in_specs=[
-            pl.BlockSpec((heads, 4, columns, depth), lambda c: (0, 0, c, 0)),
-            pl.BlockSpec((heads, 4, columns, depth), lambda c: (c, 0, 0, 0)),
+            pl.BlockSpec((heads, 4, part, depth), lambda c: (0, 0, c, 0)),
+            pl.BlockSpec((heads, 4, part, depth), lambda c: (c // PARTS, 0, c % PARTS, 0)),
         ],
-        out_specs=[pl.BlockSpec((columns, local_heads, depth), lambda c: (c, 0, 0))] * 4,
-        scratch_shapes=[pltpu.VMEM((4, columns * local_heads, depth), F32)],
+        out_specs=[pl.BlockSpec((part, local_heads, depth), lambda c: (c, 0, 0))] * 4,
+        scratch_shapes=[pltpu.VMEM((4, part * local_heads, depth), F32)],
     )(rows, cols)
     return tuple(x.reshape(shape) for x in results)
 

time: 66.4 us -> 65.2 us (0.982)
  Pallas kernels: 65.5 us -> 64.3 us
    pallas_call x1, Pallas kernels: 60.1 us -> 58.9 us  [fused(): pl.pallas_call(kernel, out_shape=[jax.ShapeDtypeStruct((heads, 4, tokens,...]
where the time goes in v3:
time: 65.2 us; the launch traced here: 65 us
  Pallas kernels  64.3 us (99%)
    pallas_call x1, Pallas kernels, fused(): pl.pallas_call(kernel, out_shape=[jax.ShapeDtypeStruct((heads, 4, tokens,...  58.9 us
    pallas_call x1, Pallas kernels, fused(): pl.pallas_call(join_kernel, grid=(QUARTERS * PARTS,), out_shape=[jax.Shap...  5.46 us

profile of v3, /device:TPU:0, one launch (start us, length us, event | category | flops | bytes accessed | tf_op | source)
XLA Modules:
  0.0 65.0 jit_solution(17984138895464365653)
XLA Ops:
  0.6 58.9 %shard_map.75 = (bf16[4,4,512,128]{3,2,1,0:T(8,128)(2,1)}, bf16[16,4,128,128]{3,2,1,0:T(8,128)(2,1)}) custom-call(bf16[512,8,128]{2,1,0:T(8,128)(2,1)} %bitcast.8, bf16[512,8,128]{2,1,0:T(8,128)(2,1)} %bitcast.9, bf16[512,8,128]{2,1,0:T(8,128)(2,1)} %bitcast.10, bf16[512,8,128]{2,1,0:T(8,128)(2,1)} %bitcast.11), custom_call_target="tpu_custom_call" | custom-call | tf_op jit(solution)/shard_map/pallas_call | solution.py:353
  59.5 5.5 %shard_map.76 = (bf16[512,8,128]{2,1,0:T(8,128)(2,1)}, bf16[512,8,128]{2,1,0:T(8,128)(2,1)}, bf16[512,8,128]{2,1,0:T(8,128)(2,1)}, bf16[512,8,128]{2,1,0:T(8,128)(2,1)}) custom-call(bf16[4,4,512,128]{3,2,1,0:T(8,128)(2,1)} %get-tuple-element.10.rows_ref, bf16[16,4,128,128]{3,2,1,0:T(8,128)(2,1)} %get-tuple-element.11.cols_ref), custom_call_target="tpu_custom_call" | custom-call | tf_op jit(solution)/shard_map/pallas_call | solution.py:377

commit v4 on v3

--- a/solution.py
+++ b/solution.py
@@ -77,7 +77,6 @@
 
 
 QUARTERS = 4
-PARTS = 1
 
 
 def each(count, body):
@@ -328,13 +327,44 @@
         each(chunks, lambda c: all_to(c).wait_send())
 
 
-def join_kernel(rows_ref, cols_ref, o_out, dq_out, dk_out, dv_out, wide):
-    columns, local_heads, depth = o_out.shape
-    for a, out in enumerate((o_out, dq_out, dk_out, dv_out)):
-        for h in range(local_heads):
-            x = rows_ref[h // 2, a] if h % 2 == 0 else cols_ref[h // 2, a]
-            wide[a, pl.ds(h, columns, stride=local_heads)] = x.astype(F32)
-        out[...] = wide[a].reshape(columns, local_heads, depth).astype(BF16)
+def join_kernel(
+    rows_ref, cols_ref, o_out, dq_out, dk_out, dv_out, rows, cols, wide, joined, arrive, leave
+):
+    tokens, local_heads, depth = o_out.shape
+    heads = local_heads // 2
+    columns = tokens // QUARTERS
+    outs = (o_out, dq_out, dk_out, dv_out)
+
+    def rows_in(quarter):
+        part = pl.ds(quarter * columns, columns)
+        return pltpu.make_async_copy(
+            rows_ref.at[:, :, part], rows.at[:, :, part], arrive.at[0, quarter]
+        )
+
+    def cols_in(quarter):
+        part = pl.ds(quarter * heads, heads)
+        return pltpu.make_async_copy(cols_ref.at[part], cols.at[part], arrive.at[1, quarter])
+
+    def out(a, quarter):
+        part = pl.ds(quarter * columns, columns)
+        return pltpu.make_async_copy(joined.at[a, part], outs[a].at[part], leave.at[a, quarter])
+
+    for quarter in range(QUARTERS):
+        rows_in(quarter).start()
+        cols_in(quarter).start()
+    for quarter in range(QUARTERS):
+        rows_in(quarter).wait()
+        cols_in(quarter).wait()
+        part = pl.ds(quarter * columns, columns)
+        for a in range(4):
+            for h in range(local_heads):
+                x = rows[h // 2, a, part] if h % 2 == 0 else cols[quarter * heads + h // 2, a]
+                wide[a, pl.ds(h, columns, stride=local_heads)] = x.astype(F32)
+            joined[a, part] = wide[a].reshape(columns, local_heads, depth).astype(BF16)
+            out(a, quarter).start()
+    for quarter in range(QUARTERS):
+        for a in range(4):
+            out(a, quarter).wait()
 
 
 def fused(queries, key_vecs, value_vecs, grad_out):
@@ -343,7 +373,6 @@
     heads = local_heads // 2
     columns = tokens // QUARTERS
     chunks = heads * QUARTERS
-    part = columns // PARTS
     flat = [x.reshape(tokens, local_heads, depth) for x in (queries, key_vecs, value_vecs, grad_out)]
     anywhere = pl.BlockSpec(memory_space=pl.ANY)
     two = pltpu.VMEM((chunks, 2, columns, depth), BF16)
@@ -376,14 +405,16 @@
     )(*flat)
     results = pl.pallas_call(
         join_kernel,
-        grid=(QUARTERS * PARTS,),
         out_shape=[jax.ShapeDtypeStruct((tokens, local_heads, depth), BF16)] * 4,
-        in_specs=[
-            pl.BlockSpec((heads, 4, part, depth), lambda c: (0, 0, c, 0)),
-            pl.BlockSpec((heads, 4, part, depth), lambda c: (c // PARTS, 0, c % PARTS, 0)),
+        in_specs=[anywhere] * 2,
+        out_specs=[anywhere] * 4,
+        scratch_shapes=[
+            row_buf, four,
+            pltpu.VMEM((4, columns * local_heads, depth), F32),
+            pltpu.VMEM((4, tokens, local_heads, depth), BF16),
+            dma((2, QUARTERS)), dma((4, QUARTERS)),
         ],
-        out_specs=[pl.BlockSpec((part, local_heads, depth), lambda c: (c, 0, 0))] * 4,
-        scratch_shapes=[pltpu.VMEM((4, part * local_heads, depth), F32)],
+        compiler_params=pltpu.CompilerParams(vmem_limit_bytes=60 * 1024 * 1024),
     )(rows, cols)
     return tuple(x.reshape(shape) for x in results)
 

time: 65.2 us -> 64.3 us (0.986)
  Pallas kernels: 64.3 us -> 63.5 us
    pallas_call x1, Pallas kernels: 5.46 us -> 4.62 us  [fused(): pl.pallas_call(join_kernel, out_shape=[jax.ShapeDtypeStruct((tokens, loca...]
where the time goes in v4:
time: 64.3 us; the launch traced here: 64.1 us
  Pallas kernels  63.5 us (99%)
    pallas_call x1, Pallas kernels, fused(): pl.pallas_call(kernel, out_shape=[jax.ShapeDtypeStruct((heads, 4, tokens,...  58.9 us
    pallas_call x1, Pallas kernels, fused(): pl.pallas_call(join_kernel, out_shape=[jax.ShapeDtypeStruct((tokens, loca...  4.62 us

profile of v4, /device:TPU:0, one launch (start us, length us, event | category | flops | bytes accessed | tf_op | source)
XLA Modules:
  0.0 64.1 jit_solution(10383991940862772239)
XLA Ops:
  0.6 58.9 %shard_map.75 = (bf16[4,4,512,128]{3,2,1,0:T(8,128)(2,1)}, bf16[16,4,128,128]{3,2,1,0:T(8,128)(2,1)}) custom-call(bf16[512,8,128]{2,1,0:T(8,128)(2,1)} %bitcast.8, bf16[512,8,128]{2,1,0:T(8,128)(2,1)} %bitcast.9, bf16[512,8,128]{2,1,0:T(8,128)(2,1)} %bitcast.10, bf16[512,8,128]{2,1,0:T(8,128)(2,1)} %bitcast.11), custom_call_target="tpu_custom_call" | custom-call | tf_op jit(solution)/shard_map/pallas_call | solution.py:382
  59.5 4.6 %shard_map.76 = (bf16[512,8,128]{2,1,0:T(8,128)(2,1)}, bf16[512,8,128]{2,1,0:T(8,128)(2,1)}, bf16[512,8,128]{2,1,0:T(8,128)(2,1)}, bf16[512,8,128]{2,1,0:T(8,128)(2,1)}) custom-call(bf16[4,4,512,128]{3,2,1,0:T(8,128)(2,1)} %get-tuple-element.10.rows_ref, bf16[16,4,128,128]{3,2,1,0:T(8,128)(2,1)} %get-tuple-element.11.cols_ref), custom_call_target="tpu_custom_call" | custom-call | tf_op jit(solution)/shard_map/pallas_call | solution.py:406
